TPU v7x, 512 devices: a whole 4x4x16 slice. The times are simulated.
512 devices in a mesh: rows: 64 (over z, y), cols: 8 (over x, core).
Axes of the slice: x: 4, y: 4, z: 16, core: 2. Of those that a mesh axis runs over, the one named last changes fastest.
Arguments:
- lower_pivot: bfloat16 [4, 2048, 4, 2048], P(None, 'rows', None, 'cols'), may hold values from -0.0625 to 0.0625
- lower_rest: bfloat16 [98304, 4, 2048], P('rows', None, 'cols'), may hold values from -0.0625 to 0.0625
- diag_inverse: bfloat16 [4, 2048, 2048], P(None, 'cols', 'rows'), may hold values from -0.125 to 0.125
- rhs_pivot: bfloat16 [4, 2048, 512], P(None, 'rows', 'cols'), may hold values from -6 to 6
- rhs_rest: bfloat16 [512, 98304], P('cols', 'rows'), may hold values from -6 to 6
Outputs:
- solution: bfloat16 [4, 2048, 512], P(None, 'cols')
- remainder: bfloat16 [512, 98304], P('cols', 'rows')
All inputs are finite; a program needn't handle non-finite values.
Results may differ from a plain program's by a relative error of at most 0.017.
Values may be sent and summed in bfloat16 or wider, within the bound.
A program may use at most 64 MiB of HBM per device.

v0:
```python
import jax
import jax.numpy as jnp
from jax import lax
from jax.sharding import PartitionSpec as P


def per_device(lower_pivot, lower_rest, diag_inverse, rhs_pivot, rhs_rest):
    block_count = lower_pivot.shape[0]
    pivot_rows = lower_pivot.shape[1]
    share_width = lower_pivot.shape[3]
    sides_share = rhs_pivot.shape[2]
    sides_total = sides_share * lax.axis_size("cols")
    rest_rows = lower_rest.shape[0]
    col_offset = lax.axis_index("cols") * sides_share
    solved = []
    for step_index in range(block_count):
        partials = jnp.zeros((pivot_rows, sides_total), jnp.float32)
        partials = lax.dynamic_update_slice(
            partials, rhs_pivot[step_index].astype(jnp.float32), (jnp.int32(0), col_offset)
        )
        if step_index > 0:
            factor_part = lower_pivot[step_index, :, :step_index, :].reshape(
                pivot_rows, step_index * share_width
            )
            known_part = jnp.concatenate(solved, axis=0)
            partials = partials - jnp.dot(
                factor_part, known_part, preferred_element_type=jnp.float32
            )
        residual = lax.psum(partials.astype(jnp.bfloat16), "cols")
        product = jnp.dot(diag_inverse[step_index], residual, preferred_element_type=jnp.float32)
        solved_block = lax.psum(product, "rows").astype(jnp.bfloat16)
        solved.append(solved_block)
    solution = jnp.stack(solved)
    flat_solution = solution.reshape(block_count * share_width, sides_total)
    flat_lower = lower_rest.reshape(rest_rows, block_count * share_width)
    total_sum = lax.psum_scatter(
        lax.dot_general(
            flat_solution, flat_lower, (((0,), (1,)), ((), ())), preferred_element_type=jnp.float32
        ).astype(jnp.bfloat16),
        "cols",
        scatter_dimension=0,
        tiled=True,
    ).astype(jnp.float32)
    remainder = (rhs_rest.astype(jnp.float32) - total_sum).astype(jnp.bfloat16)
    return (solution, remainder)


def solution(mesh):
    placed = (
        P(None, "rows", None, "cols"),
        P("rows", None, "cols"),
        P(None, "cols", "rows"),
        P(None, "rows", "cols"),
        P("cols", "rows"),
    )
    return jax.shard_map(
        per_device,
        mesh=mesh,
        in_specs=placed,
        out_specs=(P(None, "cols", None), P("cols", "rows")),
        check_vma=False,
    )
```

profile of v0, /device:TPU:1, one launch (start us, length us, event | category | flops | bytes accessed | tf_op | source)
XLA Modules:
  0.0 1294.2 jit_solution(7046899199717933439)
XLA Ops:
  7.2 0.0 copy-start
  7.2 0.0 reduce-scatter.2.cloned.1.call-start
  7.2 1.6 slice.36
  8.8 1.5 slice.39
  10.3 0.9 slice.42
  11.2 1.4 bitcast_convert_fusion.3
  12.6 0.4 dynamic_update_slice.12
  13.0 26.8 %psum.56 = bf16[32,512]{1,0:T(8,128)(2,1)S(1)} all-reduce(bf16[32,512]{1,0:T(8,128)(2,1)S(1)} %convert_element_type.62), channel_id=1, replica_groups=mesh['rows'=64,'cols'=8] {'cols'}, use_global_device_ids=true, to_apply=%region_0.0 | all-reduce | flops 16384 | bytes 65536 | tf_op jit(solution)/shard_map/psum | solution.py:29
  39.8 1.8 convolution_bitcast_fusion.4
  41.6 230.6 %all-reduce.4 = bf16[256,512]{0,1:T(8,128)(2,1)S(1)} all-reduce(f32[256,512]{0,1:T(8,128)} %convolution_bitcast_fusion.4), channel_id=1, replica_groups=mesh['rows'=64,'cols'=8] {'rows'}, use_global_device_ids=true, to_apply=%region_1.0 | all-reduce | flops 131072 | bytes 786432 | tf_op jit(solution)/shard_map/psum | solution.py:31
  272.2 1.0 dynamic_update_slice.13
  273.3 1.6 fusion.7
  274.8 79.4 %psum.58 = bf16[32,512]{1,0:T(8,128)(2,1)S(1)} all-reduce(bf16[32,512]{1,0:T(8,128)(2,1)} %fusion.7), channel_id=1, replica_groups=mesh['rows'=64,'cols'=8] {'cols'}, use_global_device_ids=true, to_apply=%region_2.0 | all-reduce | flops 16384 | bytes 65536 | tf_op jit(solution)/shard_map/psum | solution.py:29
  354.2 1.8 convolution_bitcast_fusion.3
  356.0 222.8 %all-reduce.5 = bf16[256,512]{0,1:T(8,128)(2,1)} all-reduce(f32[256,512]{0,1:T(8,128)} %convolution_bitcast_fusion.3), channel_id=1, replica_groups=mesh['rows'=64,'cols'=8] {'rows'}, use_global_device_ids=true, to_apply=%region_3.0 | all-reduce | flops 131072 | bytes 786432 | tf_op jit(solution)/shard_map/psum | solution.py:31
  578.8 1.4 copy.13
  580.2 1.0 dynamic_update_slice.14
  581.2 1.8 fusion.9
  583.0 79.2 %psum.60 = bf16[32,512]{1,0:T(8,128)(2,1)S(1)} all-reduce(bf16[32,512]{1,0:T(8,128)(2,1)} %fusion.9), channel_id=1, replica_groups=mesh['rows'=64,'cols'=8] {'cols'}, use_global_device_ids=true, to_apply=%region_4.0 | all-reduce | flops 16384 | bytes 65536 | tf_op jit(solution)/shard_map/psum | solution.py:29
  662.2 1.8 convolution_bitcast_fusion.2
  664.0 224.6 %all-reduce.6 = bf16[256,512]{0,1:T(8,128)(2,1)} all-reduce(f32[256,512]{0,1:T(8,128)} %convolution_bitcast_fusion.2), channel_id=1, replica_groups=mesh['rows'=64,'cols'=8] {'rows'}, use_global_device_ids=true, to_apply=%region_5.0 | all-reduce | flops 131072 | bytes 786432 | tf_op jit(solution)/shard_map/psum | solution.py:31
  888.6 0.4 dynamic_update_slice.15
  889.0 1.4 fusion.8
  890.4 78.8 %psum.62 = bf16[32,512]{1,0:T(8,128)(2,1)S(1)} all-reduce(bf16[32,512]{1,0:T(8,128)(2,1)S(1)} %fusion.8), channel_id=1, replica_groups=mesh['rows'=64,'cols'=8] {'cols'}, use_global_device_ids=true, to_apply=%region_6.0 | all-reduce | flops 16384 | bytes 65536 | tf_op jit(solution)/shard_map/psum | solution.py:29
  969.2 1.8 convolution_bitcast_fusion.1
  971.0 222.8 %all-reduce.7 = bf16[256,512]{0,1:T(8,128)(2,1)} all-reduce(f32[256,512]{0,1:T(8,128)} %convolution_bitcast_fusion.1), channel_id=1, replica_groups=mesh['rows'=64,'cols'=8] {'rows'}, use_global_device_ids=true, to_apply=%region_7.0 | all-reduce | flops 131072 | bytes 786432 | tf_op jit(solution)/shard_map/psum | solution.py:31
  1193.8 4.1 fusion.1
  1197.9 0.0 reduce-scatter.2.cloned.1.call-update
  1197.9 2.2 pad_maximum_fusion
  1200.1 2.3 copy.11
  1202.4 83.3 %reduce-scatter.2.cloned.1.call-done = bf16[64,1536]{1,0:T(8,128)(2,1)} async-done(((bf16[512,1536]{1,0:T(8,128)(2,1)}), bf16[64,1536]{1,0:T(8,128)(2,1)}) %reduce-scatter.2.cloned.1.call-update) | async-done | bytes 196624 | tf_op jit(solution)/shard_map/reduce_scatter | solution.py:36
  1285.7 1.6 subtract_convert_fusion
  (9 shorter events, 0.0 us)
Async XLA Ops:
  7.2 1186.6 %copy-start = (bf16[1536,4,256]{2,1,0:T(4,128)(2,1)S(1)}, bf16[1536,4,256]{2,1,0:T(4,128)(2,1)}, u32[]{:S(2)}) copy-start(bf16[1536,4,256]{2,1,0:T(4,128)(2,1)} %param.6) | copy-start | bytes 9437188
  7.2 1278.5 %reduce-scatter.2.cloned.1.call-start = ((), (), s32[]{:S(2)}) async-start(), calls=%async_computation.1 | async-start | bytes 1769472 | tf_op jit(solution)/shard_map/reduce_scatter | solution.py:36
  1200.1 85.6 %copy-start.1 = (bf16[64,1536]{1,0:T(8,128)(2,1)S(1)}, bf16[64,1536]{1,0:T(8,128)(2,1)}, u32[]{:S(2)}) copy-start(bf16[64,1536]{1,0:T(8,128)(2,1)} %param.9) | copy-start | bytes 589828
Sparse Core Ops, SparseCore 0:
  1198.0 87.6 reduce-scatter.1
where the time goes:
time: 1300 us; the launch traced here: 1290 us
  blocking collectives  1170 us (90%)
  waiting for transfers between devices  83.3 us (6%)
  matrix products  15.9 us (1%)
  between operations  14.1 us (1%)
    psum x4, blocking collectives, per_device(): solved_block = lax.psum(product, 'rows').astype(jnp.bfloat16)  901 us
    psum x4, blocking collectives, per_device(): residual = lax.psum(partials.astype(jnp.bfloat16), 'cols')  264 us
    reduce_scatter x1, waiting for transfers between devices, per_device(): lax.psum_scatter(lax.dot_general(flat_solution, flat_lower, (((0,), (1,))...  83.3 us
  transfers between devices with their start and end apart: 1, of which 1 were waited for; matrix products, arithmetic and copies ran while one was open for 0% of the time, Pallas kernels for 0%

commit v1 on v0

v1 whole, which is shorter than its diff:
```python
import functools

import jax
import jax.numpy as jnp
from jax import lax
from jax.experimental import pallas as pl
from jax.experimental.pallas import tpu as pltpu
from jax.sharding import PartitionSpec as P

MESH = pl.DeviceIdType.MESH
BF = jnp.bfloat16
F32 = jnp.float32
NZ, NY, NX = 16, 4, 4
STARTS = (0, 2, 4, 7)
LENS = (2, 2, 3, 4)
BLOCKS = 11
CONTRACT_LAST = (((1,), (1,)), ((), ()))


def dot_t(a, b):
    return lax.dot_general(a, b, CONTRACT_LAST, preferred_element_type=F32)


def kernel(own, rr, lr_hbm, sol, rem, mats, xg, lr, csend, crecv, xbuf, ybuf, fsend, frecv, rsend, rbuf,
           lsem, msend, mrecv, gsend, grecv, csem, xsem, ysem, fsem, rsem):
    r = lax.axis_index("rows")
    c = lax.axis_index("cols")
    z, y = r // NY, lax.rem(r, NY)
    x, core = c // 2, lax.rem(c, 2)

    def dev(zz, yy, xx, cc):
        return (zz * NY + yy, xx * 2 + cc)

    def zmod(v):
        return lax.rem(v + 2 * NZ, NZ)

    zdev = (dev(zmod(z + 1), y, x, core), dev(zmod(z - 1), y, x, core))
    xdev = [dev(z, y, lax.rem(x + d, NX), core) for d in (1, 2, 3)]
    ydev = [dev(z, lax.rem(y + d, NY), x, core) for d in (1, 2, 3)]
    cdev = dev(z, y, x, 1 - core)

    barrier = pltpu.get_barrier_semaphore()
    peers = [zdev[0], zdev[1], cdev] + xdev + ydev
    for p in peers:
        pl.semaphore_signal(barrier, inc=1, device_id=p, device_id_type=MESH)
    load = pltpu.make_async_copy(lr_hbm, lr, lsem.at[0])
    load.start()
    pl.semaphore_wait(barrier, len(peers))

    pending = []

    def rows_of(zz):
        return pl.ds(pl.multiple_of(zz * 32, 32), 32)

    def mat_slice(s, zz):
        return mats.at[pl.ds(STARTS[s], LENS[s]), rows_of(zz), :]

    def send_mat(s, way, k):
        src_z = zmod(z - k) if way == 0 else zmod(z + k)
        src = own.at[pl.ds(STARTS[s], LENS[s])] if k == 0 else mat_slice(s, src_z)
        cp = pltpu.make_async_remote_copy(src, mat_slice(s, src_z), msend.at[s, way, k], mrecv.at[s, way, k],
                                          device_id=zdev[way], device_id_type=MESH)
        cp.start()
        pending.append(cp)

    def wait_mat(s, way, k):
        src_z = zmod(z - k - 1) if way == 0 else zmod(z + k + 1)
        sl = mat_slice(s, src_z)
        pltpu.make_async_remote_copy(sl, sl, msend.at[s, way, k], mrecv.at[s, way, k],
                                     device_id=zdev[way], device_id_type=MESH).wait_recv()

    def relay_mat(s, k):
        for way, last in ((0, 8), (1, 7)):
            if k <= last:
                wait_mat(s, way, k - 1)
                if k < last:
                    send_mat(s, way, k)

    for s in range(4):
        for way in range(2):
            send_mat(s, way, 0)
    keep = pltpu.make_async_copy(own, mats.at[:, rows_of(z), :], lsem.at[1])
    keep.start()
    keep.wait()

    for k in range(1, 9):
        for s in range(4):
            relay_mat(s, k)

    plane_col = z // 2
    base = lax.rem(z, 2) * 32
    lane = lax.broadcasted_iota(jnp.int32, (32, 256), 1)
    row = lax.broadcasted_iota(jnp.int32, (32, 256), 0)
    owner = plane_col == c

    def pick(s):
        hit = jnp.logical_and(lane == row + (s * 64 + base), jnp.broadcast_to(owner, lane.shape))
        return jnp.where(hit, 1.0, 0.0).astype(BF)

    for s in range(4):
        part = dot_t(pick(s), mats[0])
        for t in range(s):
            part = part - dot_t(xg[z, t], mats[STARTS[s] + 1 + t])
        csend[s] = part.astype(BF)
        ccp = pltpu.make_async_remote_copy(csend.at[s], crecv.at[s], csem.at[0, s], csem.at[1, s],
                                           device_id=cdev, device_id_type=MESH)
        ccp.start()
        pending.append(ccp)
        ccp.wait_recv()
        xbuf[s, x] = (csend[s].astype(F32) + crecv[s].astype(F32)).astype(BF)
        sent = []
        for d in (1, 2, 3):
            xcp = pltpu.make_async_remote_copy(xbuf.at[s, x], xbuf.at[s, x], xsem.at[0, s, d - 1], xsem.at[1, s, d - 1],
                                               device_id=xdev[d - 1], device_id_type=MESH)
            xcp.start()
            sent.append(xcp)
        for d in (1, 2, 3):
            sl = xbuf.at[s, lax.rem(x + NX - d, NX)]
            pltpu.make_async_remote_copy(sl, sl, xsem.at[0, s, d - 1], xsem.at[1, s, d - 1],
                                         device_id=xdev[d - 1], device_id_type=MESH).wait_recv()
        pending.extend(sent)
        total = xbuf[s, 0].astype(F32)
        for i in range(1, NX):
            total = total + xbuf[s, i].astype(F32)
        prod = jnp.dot(total.astype(BF), mats[STARTS[s] if s else 1], preferred_element_type=F32)
        ybuf[s, y] = prod.astype(BF)
        sent = []
        for d in (1, 2, 3):
            ycp = pltpu.make_async_remote_copy(ybuf.at[s, y], ybuf.at[s, y], ysem.at[0, s, d - 1], ysem.at[1, s, d - 1],
                                               device_id=ydev[d - 1], device_id_type=MESH)
            ycp.start()
            sent.append(ycp)
        for d in (1, 2, 3):
            sl = ybuf.at[s, lax.rem(y + NY - d, NY)]
            pltpu.make_async_remote_copy(sl, sl, ysem.at[0, s, d - 1], ysem.at[1, s, d - 1],
                                         device_id=ydev[d - 1], device_id_type=MESH).wait_recv()
        pending.extend(sent)
        solved = ybuf[s, 0].astype(F32)
        for i in range(1, NY):
            solved = solved + ybuf[s, i].astype(F32)
        xg[z, s] = solved.astype(BF)

    def send_x(way, k):
        src_z = zmod(z - k) if way == 0 else zmod(z + k)
        cp = pltpu.make_async_remote_copy(xg.at[src_z], xg.at[src_z], gsend.at[way, k], grecv.at[way, k],
                                          device_id=zdev[way], device_id_type=MESH)
        cp.start()
        pending.append(cp)

    def wait_x(way, k):
        src_z = zmod(z - k - 1) if way == 0 else zmod(z + k + 1)
        pltpu.make_async_remote_copy(xg.at[src_z], xg.at[src_z], gsend.at[way, k], grecv.at[way, k],
                                     device_id=zdev[way], device_id_type=MESH).wait_recv()

    send_x(0, 0)
    send_x(1, 0)
    for k in range(1, 9):
        for way, last in ((0, 8), (1, 7)):
            if k <= last:
                wait_x(way, k - 1)
                if k < last:
                    send_x(way, k)
    load.wait()

    mine = pl.ds(pl.multiple_of(core * 64, 64), 64)
    other = pl.ds(pl.multiple_of((1 - core) * 64, 64), 64)
    exchanged = []
    for i, e in enumerate((2, 1, 3, 0)):
        g = lax.rem(x + e, NX)
        acc = None
        for t in range(4):
            xs = xg[pl.ds(g * 4, 4), t].reshape(128, 256)
            term = dot_t(xs, lr[:, t * 256:(t + 1) * 256])
            acc = term if acc is None else acc + term
        fsend[i] = acc.astype(BF)
        cp = pltpu.make_async_remote_copy(fsend.at[i, other], frecv.at[i], fsem.at[0, i], fsem.at[1, i],
                                          device_id=cdev, device_id_type=MESH)
        cp.start()
        exchanged.append((i, e, cp))
    final = None
    for i, e, cp in exchanged:
        cp.wait_recv()
        pending.append(cp)
        chip = fsend[i, mine].astype(F32) + frecv[i].astype(F32)
        if e:
            rsend[i] = chip.astype(BF)
            rcp = pltpu.make_async_remote_copy(rsend.at[i], rbuf.at[e - 1], rsem.at[0, e - 1], rsem.at[1, e - 1],
                                               device_id=xdev[e - 1], device_id_type=MESH)
            rcp.start()
            pending.append(rcp)
        else:
            final = chip
    for g in range(4):
        for t in range(4):
            xs = xg[g * 4:g * 4 + 4, t].reshape(128, 256)
            sol[t, :, g * 128:(g + 1) * 128] = xs.T
    for e in (1, 3, 2):
        pltpu.make_async_remote_copy(rsend.at[0], rbuf.at[e - 1], rsem.at[0, e - 1], rsem.at[1, e - 1],
                                     device_id=xdev[e - 1], device_id_type=MESH).wait_recv()
        final = final + rbuf[e - 1].astype(F32)
    rem[...] = (rr[...].astype(F32) - final).astype(BF)
    for cp in pending:
        cp.wait_send()


def per_device(lower_pivot, lower_rest, diag_inverse, rhs_pivot, rhs_rest):
    dt = jnp.swapaxes(diag_inverse, 1, 2)
    blocks = [jnp.swapaxes(rhs_pivot, 0, 1).reshape(32, 256)]
    for s in range(4):
        blocks.append(dt[s])
        for t in range(s):
            blocks.append(lower_pivot[s, :, t, :])
    own = jnp.stack(blocks)
    lr = lower_rest.reshape(1536, 1024)
    vmem = pl.BlockSpec(memory_space=pltpu.VMEM)
    dma = pltpu.SemaphoreType.DMA
    sol, rem = pl.pallas_call(
        kernel,
        out_shape=(jax.ShapeDtypeStruct((4, 256, 512), BF), jax.ShapeDtypeStruct((64, 1536), BF)),
        in_specs=[vmem, vmem, pl.BlockSpec(memory_space=pl.ANY)],
        out_specs=(vmem, vmem),
        scratch_shapes=[
            pltpu.VMEM((BLOCKS, 512, 256), BF),
            pltpu.VMEM((NZ, 4, 32, 256), BF),
            pltpu.VMEM((1536, 1024), BF),
            pltpu.VMEM((4, 32, 512), BF),
            pltpu.VMEM((4, 32, 512), BF),
            pltpu.VMEM((4, 4, 32, 512), BF),
            pltpu.VMEM((4, 4, 32, 256), BF),
            pltpu.VMEM((4, 128, 1536), BF),
            pltpu.VMEM((4, 64, 1536), BF),
            pltpu.VMEM((4, 64, 1536), BF),
            pltpu.VMEM((3, 64, 1536), BF),
            dma((2,)),
            dma((4, 2, 8)),
            dma((4, 2, 8)),
            dma((2, 8)),
            dma((2, 8)),
            dma((2, 4)),
            dma((2, 4, 3)),
            dma((2, 4, 3)),
            dma((2, 4)),
            dma((2, 3)),
        ],
        compiler_params=pltpu.CompilerParams(
            collective_id=0, has_side_effects=True, vmem_limit_bytes=48 * 1024 * 1024
        ),
        name="substitution",
    )(own, rhs_rest, lr)
    return sol, rem


def solution(mesh):
    placed = (
        P(None, "rows", None, "cols"),
        P("rows", None, "cols"),
        P(None, "cols", "rows"),
        P(None, "rows", "cols"),
        P("cols", "rows"),
    )
    return jax.shard_map(
        per_device,
        mesh=mesh,
        in_specs=placed,
        out_specs=(P(None, "cols", None), P("cols", "rows")),
        check_vma=False,
    )
```

time: 1300 us -> 135 us (0.10)
  blocking collectives: 1170 us -> 0 us
  Pallas kernels: 0 us -> 125 us
  waiting for transfers between devices: 83.3 us -> 0 us
  matrix products: 15.9 us -> 0 us
  between operations: 14.1 us -> 0.69 us
    psum x8 -> x0, blocking collectives: 1170 us -> none  [the longest x4 901 us: per_device(): solved_block = lax.psum(product, 'rows').astype(jnp.bfloat16)]
    pallas_call x0 -> x1, Pallas kernels: none -> 125 us  [per_device(): pl.pallas_call(kernel, out_shape=(jax.ShapeDtypeStruct((4, 256, 512), BF)...]
    reduce_scatter x1 -> x0, waiting for transfers between devices: 83.3 us -> none  [per_device(): lax.psum_scatter(lax.dot_general(flat_solution, flat_lower, (((0,), (1,))...]
    dot_general x8 -> x0, matrix products: 15.9 us -> none  [the longest x4 7.03 us: per_device(): jnp.dot(diag_inverse[step_index], residual, preferred_element_type=jnp.fl...]
  transfers between devices with their start and end apart: 1 -> 0, of which waited for: 1 -> 0; matrix products, arithmetic and copies ran while one was open for 0% -> 0% of each run, Pallas kernels for 0% -> 0%
where the time goes in v1:
time: 135 us; the launch traced here: 134 us
  Pallas kernels  125 us (93%)
  local copies, waits for them, and re-layouts  8.63 us (6%)
    pallas_call x1, Pallas kernels, per_device(): pl.pallas_call(kernel, out_shape=(jax.ShapeDtypeStruct((4, 256, 512), BF)...  125 us
    unnamed x14, local copies, waits for them, and re-layouts  6.57 us

profile of v1, /device:TPU:1, one launch (start us, length us, event | category | flops | bytes accessed | tf_op | source)
XLA Modules:
  0.0 134.2 jit_solution(4971822836722702320)
XLA Ops:
  0.6 0.8 copy.7
  1.4 0.1 stack_reshape.3
  1.5 0.8 slice_dynamic-update-slice_fusion
  2.3 1.2 fusion
  3.5 0.7 constant_dynamic-update-slice_fusion.6
  4.2 0.7 constant_dynamic-update-slice_fusion.3
  5.0 0.0 copy-start
  5.0 2.7 %copy.20 = bf16[192,8,4,256]{3,1,2,0:T(8,128)(2,1)S(1)} copy(bf16[192,8,4,256]{3,2,1,0:T(4,128)(2,1)} %bitcast.29) | data formatting | bytes 6291456
  7.7 0.0 copy-done
  7.7 124.8 %substitution.1 = (bf16[4,256,512]{2,1,0:T(8,128)(2,1)S(1)}, bf16[64,1536]{1,0:T(8,128)(2,1)S(1)}) custom-call(bf16[11,32,256]{2,1,0:T(8,128)(2,1)S(1)} %constant_dynamic-update-slice_fusion.own, bf16[64,1536]{1,0:T(8,128)(2,1)S(1)} %copy-done, bf16[1536,1024]{1,0:T(8,128)(2,1)S(1)} %bitcast.28), custom_call_target="tpu_custom_call" | custom-call | tf_op jit(solution)/shard_map/substitution/pallas_call | solution.py:217
  132.5 1.0 copy.50
  133.5 0.7 copy.51
  (7 shorter events, 0.0 us)
Async XLA Ops:
  5.0 2.7 %copy-start = (bf16[64,1536]{1,0:T(8,128)(2,1)S(1)}, bf16[64,1536]{1,0:T(8,128)(2,1)}, u32[]{:S(2)}) copy-start(bf16[64,1536]{1,0:T(8,128)(2,1)} %rr.1) | copy-start | bytes 589828

commit v2 on v0

v2 whole, which is shorter than its diff:
```python
import jax
import jax.numpy as jnp
from jax import lax
from jax.experimental import pallas as pl
from jax.experimental.pallas import tpu as pltpu
from jax.sharding import PartitionSpec as P

MESH = pl.DeviceIdType.MESH
BF = jnp.bfloat16
F32 = jnp.float32
NZ, NY, NX = 16, 4, 4
STARTS = (0, 1, 3, 6)
LENS = (1, 2, 3, 4)
BLOCKS = 10
OWN_HOPS = (5, -5, 2, -2, 1, -1)
CONTRACT_LAST = (((1,), (1,)), ((), ()))


def dot_t(a, b):
    return lax.dot_general(a, b, CONTRACT_LAST, preferred_element_type=F32)


def kernel(lp_hbm, dt_hbm, rp_hbm, rr_hbm, lr_hbm, sol, rem,
           lp, dt, rp, rr, lr_raw, lr, mats, bm, xg, xl, csend, crecv, xbuf, ybuf, acc, fsend, frecv, rsend, rbuf,
           lsem, msend, mrecv, wsend, wrecv, csem, xsem, ysem, qsem, fsem, rsem):
    r = lax.axis_index("rows")
    c = lax.axis_index("cols")
    z, y = r // NY, lax.rem(r, NY)
    x, core = c // 2, lax.rem(c, 2)

    def dev(zz, yy, xx, cc):
        return (zz * NY + yy, xx * 2 + cc)

    def zmod(v):
        return lax.rem(v + 2 * NZ, NZ)

    def zdev(o):
        return dev(zmod(z + o), y, x, core)

    xdev = [dev(z, y, lax.rem(x + d, NX), core) for d in (1, 2, 3)]
    ydev = [dev(z, lax.rem(y + d, NY), x, core) for d in (1, 2, 3)]
    cdev = dev(z, y, x, 1 - core)

    barrier = pltpu.get_barrier_semaphore()
    peers = [zdev(o) for o in (5, -5, 3, -3, 2, -2, 1, -1)] + xdev + ydev + [cdev]
    for p in peers:
        pl.semaphore_signal(barrier, inc=1, device_id=p, device_id_type=MESH)
    loads = [pltpu.make_async_copy(a, b, lsem.at[i]) for i, (a, b) in enumerate(
        ((rp_hbm, rp), (dt_hbm, dt), (lp_hbm, lp), (lr_hbm, lr_raw), (rr_hbm, rr)))]
    for ld in loads:
        ld.start()

    pending = []

    def rows_of(zz):
        return pl.ds(pl.multiple_of(zz * 32, 32), 32)

    def remote(src, dst, send, recv, to):
        cp = pltpu.make_async_remote_copy(src, dst, send, recv, device_id=to, device_id_type=MESH)
        cp.start()
        pending.append(cp)

    def arrive(dst, send, recv, to):
        pltpu.make_async_remote_copy(dst, dst, send, recv, device_id=to, device_id_type=MESH).wait_recv()

    def mat_slice(s, zz):
        return mats.at[pl.ds(STARTS[s], LENS[s]), rows_of(zz), :]

    def send_mat(s, way, k):
        sl = mat_slice(s, zmod(z - k) if way == 0 else zmod(z + k))
        remote(sl, sl, msend.at[s, way, k], mrecv.at[s, way, k], zdev(1 - 2 * way))

    def first(s):
        send_mat(s, 0, 0)
        send_mat(s, 1, 0)

    def relay(s, k):
        for way, last in ((0, 8), (1, 7)):
            if 1 <= k <= last:
                sl = mat_slice(s, zmod(z - k) if way == 0 else zmod(z + k))
                arrive(sl, msend.at[s, way, k - 1], mrecv.at[s, way, k - 1], zdev(1 - 2 * way))
                if k < last:
                    send_mat(s, way, k)

    quarter = pl.ds(pl.multiple_of(lax.rem(y, 2) * 16, 16), 16)

    def piece(w, zz):
        if w == 0:
            return xg.at[zz, y // 2, quarter, :]
        if w < 4:
            return xg.at[zz, w]
        return bm.at[w - 4, rows_of(zz), :] if w < 6 else mat_slice(w - 6, zz)

    def push(w, i, o, shard):
        sl = piece(w, zmod(z + shard))
        remote(sl, sl, wsend.at[w, i], wrecv.at[w, i], zdev(o))

    def got(w, i, o, shard):
        arrive(piece(w, zmod(z - o + shard)), wsend.at[w, i], wrecv.at[w, i], zdev(o))

    PASS = [(0, -5, (2, -2, 1, -1), 6), (1, 5, (-3, -2, 2, -1, 1), 10)]

    def wave_a(w):
        for i, o in enumerate(OWN_HOPS):
            push(w, i, o, 0)

    def wave_b(w):
        for i, shard, hops, base in PASS:
            got(w, i, OWN_HOPS[i], 0)
            for j, o in enumerate(hops):
                push(w, base + j, o, shard)

    def wave_c(w):
        for i in range(2, 6):
            got(w, i, OWN_HOPS[i], 0)
        for i, shard, hops, base in PASS:
            for j, o in enumerate(hops):
                got(w, base + j, o, shard)

    base_n = lax.rem(z, 2) * 32
    lane = lax.broadcasted_iota(jnp.int32, (32, 128), 1)
    row = lax.broadcasted_iota(jnp.int32, (32, 128), 0)
    owner = z // 2 == c

    def pick(s):
        hit = jnp.logical_and(lane == row + ((s % 2) * 64 + base_n), jnp.broadcast_to(owner, lane.shape))
        return jnp.where(hit, 1.0, 0.0).astype(BF)

    def step_p(s):
        part = dot_t(pick(s), bm[s // 2])
        for t in range(s):
            part = part - dot_t(xl[t], mats[STARTS[s] + 1 + t])
        csend[s] = part.astype(BF)
        remote(csend.at[s], crecv.at[s], csem.at[0, s], csem.at[1, s], cdev)

    def step_x(s):
        arrive(crecv.at[s], csem.at[0, s], csem.at[1, s], cdev)
        xbuf[s, x] = (csend[s].astype(F32) + crecv[s].astype(F32)).astype(BF)
        for d in (2, 1, 3):
            remote(xbuf.at[s, x], xbuf.at[s, x], xsem.at[0, s, d - 1], xsem.at[1, s, d - 1], xdev[d - 1])

    def step_y(s):
        for d in (1, 3, 2):
            arrive(xbuf.at[s, lax.rem(x + NX - d, NX)], xsem.at[0, s, d - 1], xsem.at[1, s, d - 1], xdev[d - 1])
        total = xbuf[s, 0].astype(F32)
        for i in range(1, NX):
            total = total + xbuf[s, i].astype(F32)
        prod = jnp.dot(total.astype(BF), mats[STARTS[s]], preferred_element_type=F32)
        ybuf[s, y] = prod.astype(BF)
        for d in (2, 1, 3):
            remote(ybuf.at[s, y], ybuf.at[s, y], ysem.at[0, s, d - 1], ysem.at[1, s, d - 1], ydev[d - 1])

    def step_z(s):
        for d in (1, 3, 2):
            arrive(ybuf.at[s, lax.rem(y + NY - d, NY)], ysem.at[0, s, d - 1], ysem.at[1, s, d - 1], ydev[d - 1])
        solved = ybuf[s, 0].astype(F32)
        for i in range(1, NY):
            solved = solved + ybuf[s, i].astype(F32)
        xl[s] = solved.astype(BF)
        if s == 1:
            xg[z, y // 2, quarter, :] = xl[y // 2, quarter, :]
            wave_a(0)
        elif s > 1:
            xg[z, s] = xl[s]
            wave_a(s)

    def share_slice(yy):
        return xg.at[:, yy // 2, pl.ds(pl.multiple_of(lax.rem(yy, 2) * 16, 16), 16), :]

    def share():
        for d in (2, 1, 3):
            remote(share_slice(y), share_slice(y), qsem.at[0, d - 1], qsem.at[1, d - 1], ydev[d - 1])

    def shared():
        for d in (1, 3, 2):
            arrive(share_slice(lax.rem(y + NY - d, NY)), qsem.at[0, d - 1], qsem.at[1, d - 1], ydev[d - 1])

    def tile(i):
        rows = pl.ds(i * 128, 128)
        for t in range(4):
            lr[rows, t * 256:(t + 1) * 256] = lr_raw[rows, t, :]

    loads[0].wait()
    for s in range(4):
        bm[s // 2, rows_of(z), (s % 2) * 64:(s % 2) * 64 + 64] = rp[s]
    loads[1].wait()
    loads[2].wait()
    for s in range(4):
        mats[STARTS[s], rows_of(z), :] = dt[s]
        for t in range(s):
            mats[STARTS[s] + 1 + t, rows_of(z), :] = lp[s, :, t, :]
    pl.semaphore_wait(barrier, len(peers))

    wave_a(4)
    wave_a(6)
    first(2)
    loads[3].wait()
    tile(0)
    tile(1)
    tile(2)
    tile(3)
    wave_b(4)
    wave_b(6)
    wave_a(7)
    relay(2, 1)
    first(3)
    tile(4)
    tile(5)
    tile(6)
    wave_c(4)
    step_p(0)
    relay(2, 2)
    step_x(0)
    wave_b(7)
    relay(3, 1)
    wave_c(6)
    step_y(0)
    wave_a(5)
    relay(2, 3)
    relay(3, 2)
    step_z(0)
    wave_c(7)
    step_p(1)
    relay(2, 4)
    step_x(1)
    wave_b(5)
    relay(3, 3)
    relay(2, 5)
    step_y(1)
    relay(3, 4)
    relay(2, 6)
    step_z(1)
    relay(2, 7)
    relay(3, 5)
    relay(2, 8)
    wave_c(5)
    step_p(2)
    relay(3, 6)
    step_x(2)
    wave_b(0)
    relay(3, 7)
    tile(7)
    tile(8)
    step_y(2)
    relay(3, 8)
    step_z(2)
    step_p(3)
    wave_c(0)
    share()
    tile(9)
    step_x(3)
    tile(10)
    tile(11)
    step_y(3)
    wave_b(2)
    step_z(3)
    shared()
    for i in range(4):
        rows = pl.ds(i * 128, 128)
        part = None
        for t in range(2):
            term = dot_t(xg[i * 4:i * 4 + 4, t].reshape(128, 256), lr[:, t * 256:(t + 1) * 256])
            part = term if part is None else part + term
        acc[rows, :] = part
    for g in range(4):
        for t in range(2):
            sol[t, :, g * 128:(g + 1) * 128] = xg[g * 4:g * 4 + 4, t].reshape(128, 256).T
    wave_b(3)
    wave_c(2)
    for i in range(4):
        rows = pl.ds(i * 128, 128)
        acc[rows, :] += dot_t(xg[i * 4:i * 4 + 4, 2].reshape(128, 256), lr[:, 512:768])
    for g in range(4):
        sol[2, :, g * 128:(g + 1) * 128] = xg[g * 4:g * 4 + 4, 2].reshape(128, 256).T
    wave_c(3)

    mine = pl.ds(pl.multiple_of(core * 64, 64), 64)
    other = pl.ds(pl.multiple_of((1 - core) * 64, 64), 64)
    order = (2, 1, 3, 0)
    for i, e in enumerate(order):
        g = lax.rem(x + e, NX)
        rows = pl.ds(pl.multiple_of(g * 128, 128), 128)
        part = acc[rows, :] + dot_t(xg[pl.ds(g * 4, 4), 3].reshape(128, 256), lr[:, 768:1024])
        fsend[i] = part.astype(BF)
        remote(fsend.at[i, other], frecv.at[i], fsem.at[0, i], fsem.at[1, i], cdev)
    final = None
    for i, e in enumerate(order):
        arrive(frecv.at[i], fsem.at[0, i], fsem.at[1, i], cdev)
        chip = fsend[i, mine].astype(F32) + frecv[i].astype(F32)
        if e:
            rsend[i] = chip.astype(BF)
            remote(rsend.at[i], rbuf.at[e - 1], rsem.at[0, e - 1], rsem.at[1, e - 1], xdev[e - 1])
        else:
            loads[4].wait()
            final = rr[...].astype(F32) - chip
    for g in range(4):
        sol[3, :, g * 128:(g + 1) * 128] = xg[g * 4:g * 4 + 4, 3].reshape(128, 256).T
    for e in (1, 3, 2):
        arrive(rbuf.at[e - 1], rsem.at[0, e - 1], rsem.at[1, e - 1], xdev[e - 1])
        final = final - rbuf[e - 1].astype(F32)
    rem[...] = final.astype(BF)
    for cp in pending:
        cp.wait_send()


def per_device(lower_pivot, lower_rest, diag_inverse, rhs_pivot, rhs_rest):
    vmem = pl.BlockSpec(memory_space=pltpu.VMEM)
    hbm = pl.BlockSpec(memory_space=pl.ANY)
    dma = pltpu.SemaphoreType.DMA
    return pl.pallas_call(
        kernel,
        out_shape=(jax.ShapeDtypeStruct((4, 256, 512), BF), jax.ShapeDtypeStruct((64, 1536), BF)),
        in_specs=[hbm] * 5,
        out_specs=(vmem, vmem),
        scratch_shapes=[
            pltpu.VMEM((4, 32, 4, 256), BF),
            pltpu.VMEM((4, 32, 256), BF),
            pltpu.VMEM((4, 32, 64), BF),
            pltpu.VMEM((64, 1536), BF),
            pltpu.VMEM((1536, 4, 256), BF),
            pltpu.VMEM((1536, 1024), BF),
            pltpu.VMEM((BLOCKS, 512, 256), BF),
            pltpu.VMEM((2, 512, 128), BF),
            pltpu.VMEM((NZ, 4, 32, 256), BF),
            pltpu.VMEM((4, 32, 256), BF),
            pltpu.VMEM((4, 32, 512), BF),
            pltpu.VMEM((4, 32, 512), BF),
            pltpu.VMEM((4, 4, 32, 512), BF),
            pltpu.VMEM((4, 4, 32, 256), BF),
            pltpu.VMEM((512, 1536), F32),
            pltpu.VMEM((4, 128, 1536), BF),
            pltpu.VMEM((4, 64, 1536), BF),
            pltpu.VMEM((3, 64, 1536), BF),
            pltpu.VMEM((3, 64, 1536), BF),
            dma((5,)),
            dma((4, 2, 8)),
            dma((4, 2, 8)),
            dma((8, 15)),
            dma((8, 15)),
            dma((2, 4)),
            dma((2, 4, 3)),
            dma((2, 4, 3)),
            dma((2, 3)),
            dma((2, 4)),
            dma((2, 3)),
        ],
        compiler_params=pltpu.CompilerParams(
            collective_id=0, has_side_effects=True, vmem_limit_bytes=63 * 1024 * 1024
        ),
        name="substitution",
    )(lower_pivot, jnp.swapaxes(diag_inverse, 1, 2), rhs_pivot, rhs_rest, lower_rest)


def solution(mesh):
    placed = (
        P(None, "rows", None, "cols"),
        P("rows", None, "cols"),
        P(None, "cols", "rows"),
        P(None, "rows", "cols"),
        P("cols", "rows"),
    )
    return jax.shard_map(
        per_device,
        mesh=mesh,
        in_specs=placed,
        out_specs=(P(None, "cols", None), P("cols", "rows")),
        check_vma=False,
    )
```

time: 1300 us -> 114 us (0.09)
  blocking collectives: 1170 us -> 0 us
  Pallas kernels: 0 us -> 110 us
  waiting for transfers between devices: 83.3 us -> 0 us
  matrix products: 15.9 us -> 0 us
  between operations: 14.1 us -> 0.64 us
    psum x8 -> x0, blocking collectives: 1170 us -> none  [the longest x4 901 us: per_device(): solved_block = lax.psum(product, 'rows').astype(jnp.bfloat16)]
    pallas_call x0 -> x1, Pallas kernels: none -> 110 us  [per_device(): pl.pallas_call(kernel, out_shape=(jax.ShapeDtypeStruct((4, 256, 512), BF)...]
    reduce_scatter x1 -> x0, waiting for transfers between devices: 83.3 us -> none  [per_device(): lax.psum_scatter(lax.dot_general(flat_solution, flat_lower, (((0,), (1,))...]
    dot_general x8 -> x0, matrix products: 15.9 us -> none  [the longest x4 7.03 us: per_device(): jnp.dot(diag_inverse[step_index], residual, preferred_element_type=jnp.fl...]
  transfers between devices with their start and end apart: 1 -> 0, of which waited for: 1 -> 0; matrix products, arithmetic and copies ran while one was open for 0% -> 0% of each run, Pallas kernels for 0% -> 0%
where the time goes in v2:
time: 114 us
  Pallas kernels  110 us (96%)
  local copies, waits for them, and re-layouts  3.88 us (3%)
    pallas_call x1, Pallas kernels, per_device(): pl.pallas_call(kernel, out_shape=(jax.ShapeDtypeStruct((4, 256, 512), BF)...  110 us
    unnamed x2, local copies, waits for them, and re-layouts  3.88 us

profile of v2, /device:TPU:1, one launch (start us, length us, event | category | flops | bytes accessed | tf_op | source)
XLA Modules:
  0.0 114.1 jit_solution(11777970840657086259)
XLA Ops:
  0.6 109.6 %substitution.1 = (bf16[4,256,512]{2,1,0:T(8,128)(2,1)}, bf16[64,1536]{1,0:T(8,128)(2,1)}) custom-call(bf16[4,32,4,256]{3,2,1,0:T(4,128)(2,1)} %lp_hbm.1, bf16[4,32,256]{2,1,0:T(8,128)(2,1)} %bitcast.1, bf16[4,32,64]{2,1,0:T(8,128)(2,1)} %rp_hbm.1, bf16[64,1536]{1,0:T(8,128)(2,1)} %rr_hbm.1, bf16[1536,4,256]{2,1,0:T(4,128)(2,1)} %lr_hbm.1), custom_call_target="tpu_custom_call" | custom-call | tf_op jit(solution)/shard_map/substitution/pallas_call | solution.py:310
  110.3 2.3 %copy.9 = bf16[4,256,512]{2,1,0:T(8,128)(2,1)} copy(bf16[4,256,512]{2,1,0:T(8,128)(2,1)} %get-tuple-element.4) | data formatting | bytes 2097152
  112.5 1.6 %copy.10 = bf16[64,1536]{1,0:T(8,128)(2,1)} copy(bf16[64,1536]{1,0:T(8,128)(2,1)} %get-tuple-element.5) | data formatting | bytes 393216

commit v3 on v2

--- a/solution.py
+++ b/solution.py
@@ -193,7 +193,9 @@
 
     wave_a(4)
     wave_a(6)
+    first(1)
     first(2)
+    first(3)
     loads[3].wait()
     tile(0)
     tile(1)
@@ -201,57 +203,61 @@
     tile(3)
     wave_b(4)
     wave_b(6)
-    wave_a(7)
+    relay(1, 1)
     relay(2, 1)
-    first(3)
+    relay(3, 1)
     tile(4)
+    relay(1, 2)
+    relay(2, 2)
+    relay(3, 2)
     tile(5)
-    tile(6)
     wave_c(4)
     step_p(0)
-    relay(2, 2)
+    relay(1, 3)
+    relay(2, 3)
+    relay(3, 3)
     step_x(0)
-    wave_b(7)
-    relay(3, 1)
+    relay(1, 4)
+    relay(2, 4)
+    relay(3, 4)
     wave_c(6)
     step_y(0)
+    relay(1, 5)
+    relay(2, 5)
+    relay(3, 5)
+    step_z(0)
+    relay(1, 6)
+    relay(2, 6)
+    relay(3, 6)
     wave_a(5)
-    relay(2, 3)
-    relay(3, 2)
-    step_z(0)
-    wave_c(7)
+    relay(1, 7)
+    relay(2, 7)
+    relay(3, 7)
+    relay(1, 8)
     step_p(1)
-    relay(2, 4)
+    wave_b(5)
     step_x(1)
-    wave_b(5)
-    relay(3, 3)
-    relay(2, 5)
+    tile(6)
+    tile(7)
     step_y(1)
-    relay(3, 4)
-    relay(2, 6)
-    step_z(1)
-    relay(2, 7)
-    relay(3, 5)
     relay(2, 8)
     wave_c(5)
+    step_z(1)
     step_p(2)
-    relay(3, 6)
+    tile(8)
     step_x(2)
     wave_b(0)
-    relay(3, 7)
-    tile(7)
-    tile(8)
+    tile(9)
     step_y(2)
     relay(3, 8)
     step_z(2)
     step_p(3)
+    tile(10)
+    step_x(3)
+    tile(11)
+    step_y(3)
     wave_c(0)
     share()
-    tile(9)
-    step_x(3)
-    tile(10)
-    tile(11)
-    step_y(3)
     wave_b(2)
     step_z(3)
     shared()
@@ -277,22 +283,24 @@
     mine = pl.ds(pl.multiple_of(core * 64, 64), 64)
     other = pl.ds(pl.multiple_of((1 - core) * 64, 64), 64)
     order = (2, 1, 3, 0)
-    for i, e in enumerate(order):
-        g = lax.rem(x + e, NX)
-        rows = pl.ds(pl.multiple_of(g * 128, 128), 128)
-        part = acc[rows, :] + dot_t(xg[pl.ds(g * 4, 4), 3].reshape(128, 256), lr[:, 768:1024])
-        fsend[i] = part.astype(BF)
-        remote(fsend.at[i, other], frecv.at[i], fsem.at[0, i], fsem.at[1, i], cdev)
     final = None
-    for i, e in enumerate(order):
-        arrive(frecv.at[i], fsem.at[0, i], fsem.at[1, i], cdev)
-        chip = fsend[i, mine].astype(F32) + frecv[i].astype(F32)
-        if e:
-            rsend[i] = chip.astype(BF)
-            remote(rsend.at[i], rbuf.at[e - 1], rsem.at[0, e - 1], rsem.at[1, e - 1], xdev[e - 1])
-        else:
-            loads[4].wait()
-            final = rr[...].astype(F32) - chip
+    for j in range(5):
+        if j < 4:
+            g = lax.rem(x + order[j], NX)
+            rows = pl.ds(pl.multiple_of(g * 128, 128), 128)
+            part = acc[rows, :] + dot_t(xg[pl.ds(g * 4, 4), 3].reshape(128, 256), lr[:, 768:1024])
+            fsend[j] = part.astype(BF)
+            remote(fsend.at[j, other], frecv.at[j], fsem.at[0, j], fsem.at[1, j], cdev)
+        if j:
+            i, e = j - 1, order[j - 1]
+            arrive(frecv.at[i], fsem.at[0, i], fsem.at[1, i], cdev)
+            chip = fsend[i, mine].astype(F32) + frecv[i].astype(F32)
+            if e:
+                rsend[i] = chip.astype(BF)
+                remote(rsend.at[i], rbuf.at[e - 1], rsem.at[0, e - 1], rsem.at[1, e - 1], xdev[e - 1])
+            else:
+                loads[4].wait()
+                final = rr[...].astype(F32) - chip
     for g in range(4):
         sol[3, :, g * 128:(g + 1) * 128] = xg[g * 4:g * 4 + 4, 3].reshape(128, 256).T
     for e in (1, 3, 2):
@@ -305,7 +313,7 @@
 
 def per_device(lower_pivot, lower_rest, diag_inverse, rhs_pivot, rhs_rest):
     vmem = pl.BlockSpec(memory_space=pltpu.VMEM)
-    hbm = pl.BlockSpec(memory_space=pl.ANY)
+    hbm = pl.BlockSpec(memory_space=pltpu.HBM)
     dma = pltpu.SemaphoreType.DMA
     return pl.pallas_call(
         kernel,

time: 114 us -> 117 us (1.026)
  Pallas kernels: 110 us -> 112 us
    pallas_call x1, Pallas kernels: 110 us -> 112 us  [per_device(): pl.pallas_call(kernel, out_shape=(jax.ShapeDtypeStruct((4, 256, 512), BF)...]
where the time goes in v3:
time: 117 us; the launch traced here: 116 us
  Pallas kernels  112 us (96%)
  local copies, waits for them, and re-layouts  3.88 us (3%)
    pallas_call x1, Pallas kernels, per_device(): pl.pallas_call(kernel, out_shape=(jax.ShapeDtypeStruct((4, 256, 512), BF)...  112 us
    unnamed x2, local copies, waits for them, and re-layouts  3.88 us

profile of v3, /device:TPU:1, one launch (start us, length us, event | category | flops | bytes accessed | tf_op | source)
XLA Modules:
  0.0 116.4 jit_solution(14712939495752202632)
XLA Ops:
  0.6 111.9 %substitution.1 = (bf16[4,256,512]{2,1,0:T(8,128)(2,1)}, bf16[64,1536]{1,0:T(8,128)(2,1)}) custom-call(bf16[4,32,4,256]{3,2,1,0:T(4,128)(2,1)} %lp_hbm.1, bf16[4,32,256]{2,1,0:T(8,128)(2,1)} %bitcast.1, bf16[4,32,64]{2,1,0:T(8,128)(2,1)} %rp_hbm.1, bf16[64,1536]{1,0:T(8,128)(2,1)} %rr_hbm.1, bf16[1536,4,256]{2,1,0:T(4,128)(2,1)} %lr_hbm.1), custom_call_target="tpu_custom_call" | custom-call | tf_op jit(solution)/shard_map/substitution/pallas_call | solution.py:318
  112.5 2.3 %copy.9 = bf16[4,256,512]{2,1,0:T(8,128)(2,1)} copy(bf16[4,256,512]{2,1,0:T(8,128)(2,1)} %get-tuple-element.4) | data formatting | bytes 2097152
  114.8 1.6 %copy.10 = bf16[64,1536]{1,0:T(8,128)(2,1)} copy(bf16[64,1536]{1,0:T(8,128)(2,1)} %get-tuple-element.5) | data formatting | bytes 393216

commit v4 on v2

--- a/solution.py
+++ b/solution.py
@@ -262,39 +262,37 @@
             term = dot_t(xg[i * 4:i * 4 + 4, t].reshape(128, 256), lr[:, t * 256:(t + 1) * 256])
             part = term if part is None else part + term
         acc[rows, :] = part
-    for g in range(4):
-        for t in range(2):
-            sol[t, :, g * 128:(g + 1) * 128] = xg[g * 4:g * 4 + 4, t].reshape(128, 256).T
     wave_b(3)
     wave_c(2)
     for i in range(4):
         rows = pl.ds(i * 128, 128)
         acc[rows, :] += dot_t(xg[i * 4:i * 4 + 4, 2].reshape(128, 256), lr[:, 512:768])
-    for g in range(4):
-        sol[2, :, g * 128:(g + 1) * 128] = xg[g * 4:g * 4 + 4, 2].reshape(128, 256).T
     wave_c(3)
 
     mine = pl.ds(pl.multiple_of(core * 64, 64), 64)
     other = pl.ds(pl.multiple_of((1 - core) * 64, 64), 64)
     order = (2, 1, 3, 0)
-    for i, e in enumerate(order):
-        g = lax.rem(x + e, NX)
-        rows = pl.ds(pl.multiple_of(g * 128, 128), 128)
-        part = acc[rows, :] + dot_t(xg[pl.ds(g * 4, 4), 3].reshape(128, 256), lr[:, 768:1024])
-        fsend[i] = part.astype(BF)
-        remote(fsend.at[i, other], frecv.at[i], fsem.at[0, i], fsem.at[1, i], cdev)
     final = None
-    for i, e in enumerate(order):
-        arrive(frecv.at[i], fsem.at[0, i], fsem.at[1, i], cdev)
-        chip = fsend[i, mine].astype(F32) + frecv[i].astype(F32)
-        if e:
-            rsend[i] = chip.astype(BF)
-            remote(rsend.at[i], rbuf.at[e - 1], rsem.at[0, e - 1], rsem.at[1, e - 1], xdev[e - 1])
-        else:
-            loads[4].wait()
-            final = rr[...].astype(F32) - chip
+    for j in range(5):
+        if j < 4:
+            g = lax.rem(x + order[j], NX)
+            rows = pl.ds(pl.multiple_of(g * 128, 128), 128)
+            part = acc[rows, :] + dot_t(xg[pl.ds(g * 4, 4), 3].reshape(128, 256), lr[:, 768:1024])
+            fsend[j] = part.astype(BF)
+            remote(fsend.at[j, other], frecv.at[j], fsem.at[0, j], fsem.at[1, j], cdev)
+        if j:
+            i, e = j - 1, order[j - 1]
+            arrive(frecv.at[i], fsem.at[0, i], fsem.at[1, i], cdev)
+            chip = fsend[i, mine].astype(F32) + frecv[i].astype(F32)
+            if e:
+                rsend[i] = chip.astype(BF)
+                remote(rsend.at[i], rbuf.at[e - 1], rsem.at[0, e - 1], rsem.at[1, e - 1], xdev[e - 1])
+            else:
+                loads[4].wait()
+                final = rr[...].astype(F32) - chip
     for g in range(4):
-        sol[3, :, g * 128:(g + 1) * 128] = xg[g * 4:g * 4 + 4, 3].reshape(128, 256).T
+        for t in range(4):
+            sol[t, :, g * 128:(g + 1) * 128] = xg[g * 4:g * 4 + 4, t].reshape(128, 256).T
     for e in (1, 3, 2):
         arrive(rbuf.at[e - 1], rsem.at[0, e - 1], rsem.at[1, e - 1], xdev[e - 1])
         final = final - rbuf[e - 1].astype(F32)
@@ -305,7 +303,7 @@
 
 def per_device(lower_pivot, lower_rest, diag_inverse, rhs_pivot, rhs_rest):
     vmem = pl.BlockSpec(memory_space=pltpu.VMEM)
-    hbm = pl.BlockSpec(memory_space=pl.ANY)
+    hbm = pl.BlockSpec(memory_space=pltpu.HBM)
     dma = pltpu.SemaphoreType.DMA
     return pl.pallas_call(
         kernel,

time: 114 us -> 114 us (level)
  no operation moved by 1% of the time
where the time goes in v4:
time: 114 us
  Pallas kernels  109 us (96%)
  local copies, waits for them, and re-layouts  3.88 us (3%)
    pallas_call x1, Pallas kernels, per_device(): pl.pallas_call(kernel, out_shape=(jax.ShapeDtypeStruct((4, 256, 512), BF)...  109 us
    unnamed x2, local copies, waits for them, and re-layouts  3.88 us

profile of v4, /device:TPU:1, one launch (start us, length us, event | category | flops | bytes accessed | tf_op | source)
XLA Modules:
  0.0 113.7 jit_solution(5817481289170560439)
XLA Ops:
  0.6 109.2 %substitution.1 = (bf16[4,256,512]{2,1,0:T(8,128)(2,1)}, bf16[64,1536]{1,0:T(8,128)(2,1)}) custom-call(bf16[4,32,4,256]{3,2,1,0:T(4,128)(2,1)} %lp_hbm.1, bf16[4,32,256]{2,1,0:T(8,128)(2,1)} %bitcast.1, bf16[4,32,64]{2,1,0:T(8,128)(2,1)} %rp_hbm.1, bf16[64,1536]{1,0:T(8,128)(2,1)} %rr_hbm.1, bf16[1536,4,256]{2,1,0:T(4,128)(2,1)} %lr_hbm.1), custom_call_target="tpu_custom_call" | custom-call | tf_op jit(solution)/shard_map/substitution/pallas_call | solution.py:308
  109.8 2.3 %copy.9 = bf16[4,256,512]{2,1,0:T(8,128)(2,1)} copy(bf16[4,256,512]{2,1,0:T(8,128)(2,1)} %get-tuple-element.4) | data formatting | bytes 2097152
  112.1 1.6 %copy.10 = bf16[64,1536]{1,0:T(8,128)(2,1)} copy(bf16[64,1536]{1,0:T(8,128)(2,1)} %get-tuple-element.5) | data formatting | bytes 393216
